TPU v7x, 512 devices: a whole 4x8x8 slice. The times are simulated.
512 devices in a mesh: wide: 64 (over y, x, core), narrow: 8 (over z).
Axes of the slice: x: 4, y: 8, z: 8, core: 2. Of those that a mesh axis runs over, the one named last changes fastest.
Arguments:
- matrix_slab: float32 [16, 4194304], P(None, ('wide', 'narrow')), may hold values from -6 to 6
- row_signs: int32 [4194304], P(('wide', 'narrow')), may hold values from -1 to 1, as said below
- sample_rows: int32 [524288], P(('wide', 'narrow')), may hold values from 0 to 7, as said below
Outputs:
- sketch: float32 [16, 524288], P(None, ('wide', 'narrow'))
- sketch_gram: float32 [16, 16], replicated
Inputs may be any that keep to these rules, and one draw needn't show every extreme that they name: `row_signs`: each entry is +1 or -1. `sample_rows`: entry k is the offset of the k-th sampled row inside the run of 8 rows that starts at k * 8.
All inputs are finite; a program needn't handle non-finite values.
Results may differ from a plain program's by a relative error of at most 0.00013.
Values sent between devices are 32-bit elements; how exact they have to be, the bound alone decides.
A program may use at most 64 MiB of HBM per device.

v0:
```python
import math

import jax
import jax.numpy as jnp
from jax import lax
from jax.sharding import PartitionSpec as P


def from_partner(value, axis, apart):
    mask = 2**apart
    pairs = [(source, source ^ mask) for source in range(lax.axis_size(axis))]
    return lax.ppermute(value, axis, pairs)


def sylvester(order_size):
    series = lax.iota(jnp.int32, order_size)
    common_bits = series[:, None] & series[None, :]
    parity = jnp.zeros_like(common_bits)
    for bit_pos in range(order_size.bit_length() - 1):
        parity = parity ^ common_bits >> bit_pos & 1
    return (1 - 2 * parity).astype(jnp.float32)


def narrow_section(values):
    axis_width = lax.axis_size("narrow")
    position = lax.axis_index("narrow")
    for bit_pos in range(axis_width.bit_length() - 1):
        partner = from_partner(values, "narrow", bit_pos)
        own_bit = position >> bit_pos & 1
        values = jnp.where(own_bit == 0, values + partner, partner - values)
    return values


def pick_samples(values, sample_rows):
    sample_count = sample_rows.shape[0]
    run_length = values.shape[1] // sample_count
    local_rows = lax.iota(jnp.int32, sample_count) * run_length + sample_rows
    return jnp.take(values, local_rows, axis=1)


def wide_section(values, sample_rows):
    axis_width = lax.axis_size("wide")
    columns, row_count = values.shape
    hadamard = sylvester(axis_width)
    blocked = values.reshape(columns, axis_width, row_count // axis_width)
    mixed_rows = jnp.einsum(
        "ms,csr->cmr",
        hadamard,
        lax.all_to_all(blocked, "wide", split_axis=1, concat_axis=1, tiled=True),
        precision=lax.Precision.HIGHEST,
    )
    result = lax.all_to_all(mixed_rows, "wide", split_axis=1, concat_axis=1, tiled=True)
    result = result.reshape(columns, row_count)
    return pick_samples(result, sample_rows)


def shards(matrix_slab, row_signs, sample_rows):
    values = matrix_slab * row_signs.astype(jnp.float32)[None, :]
    columns, row_count = values.shape
    inner_table = sylvester(128)
    outer_table = sylvester(row_count // 128)
    tiles = values.reshape(columns, row_count // 128, 128)
    tiles = jnp.einsum("cqt,ts->cqs", tiles, inner_table, precision=lax.Precision.HIGHEST)
    tiles = jnp.einsum("pq,cqs->cps", outer_table, tiles, precision=lax.Precision.HIGHEST)
    values = tiles.reshape(columns, row_count)
    values = narrow_section(values)
    picked_rows = wide_section(values, sample_rows)
    devices_all = lax.axis_size("wide") * lax.axis_size("narrow")
    sketch = picked_rows * jnp.float32(1.0 / math.sqrt(row_count * devices_all))
    sample_count = sample_rows.shape[0]
    partial_gram = jnp.dot(
        sketch, sketch.T, precision=lax.Precision.HIGHEST, preferred_element_type=jnp.float32
    ) / jnp.float32(sample_count * devices_all)
    sketch_gram = lax.psum(partial_gram, ("wide", "narrow"))
    return (sketch, sketch_gram)


def solution(mesh):
    in_specs = (P(None, ("wide", "narrow")), P(("wide", "narrow")), P(("wide", "narrow")))
    out_specs = (P(None, ("wide", "narrow")), P())
    return jax.shard_map(shards, mesh=mesh, in_specs=in_specs, out_specs=out_specs, check_vma=False)
```

profile of v0, /device:TPU:1, one launch (start us, length us, event | category | flops | bytes accessed | tf_op | source)
XLA Modules:
  0.0 241.7 jit_solution(14482409116508778793)
XLA Ops:
  0.6 0.8 convert_element_type.12
  1.4 1.1 multiply_bitcast_fusion
  2.5 0.1 copy.17
  2.6 0.6 fusion.5
  3.2 0.6 fusion.34
  3.8 0.3 copy.25
  4.1 4.8 %collective-permute-start = (f32[16,8192]{1,0:T(8,128)S(1)}, f32[16,8192]{1,0:T(8,128)S(1)}, u32[]{:S(2)}, u32[]{:S(2)}) collective-permute-start(f32[16,8192]{1,0:T(8,128)S(1)} %bitcast.34), channel_id=1, source_target_pairs={{0,1},{1,0},{2,3},{3,2},{4,5},{5,4},{6,7},{7,6},{8,9},{9,8},{10,11... | collective-permute-start | bytes 1572872 | tf_op jit(solution)/shard_map/ppermute | solution.py:12
  9.0 0.0 copy-start
  9.0 7.5 %collective-permute-done = f32[16,8192]{1,0:T(8,128)S(1)} collective-permute-done((f32[16,8192]{1,0:T(8,128)S(1)}, f32[16,8192]{1,0:T(8,128)S(1)}, u32[]{:S(2)}, u32[]{:S(2)}) %collective-permute-start) | collective-permute-done | bytes 524320 | tf_op jit(solution)/shard_map/ppermute | solution.py:12
  16.5 0.3 subtract_select_fusion.1
  16.8 9.9 %collective-permute-start.1 = (f32[16,8192]{1,0:T(8,128)S(1)}, f32[16,8192]{1,0:T(8,128)S(1)}, u32[]{:S(2)}, u32[]{:S(2)}) collective-permute-start(f32[16,8192]{1,0:T(8,128)S(1)} %subtract_select_fusion.1), channel_id=1, source_target_pairs={{0,2},{1,3},{2,0},{3,1},{4,6},{5,7},{6,4},{7,5},{8,10},{9,11},{10,... | collective-permute-start | bytes 1572872 | tf_op jit(solution)/shard_map/ppermute | solution.py:12
  26.8 22.7 %collective-permute-done.1 = f32[16,8192]{1,0:T(8,128)S(1)} collective-permute-done((f32[16,8192]{1,0:T(8,128)S(1)}, f32[16,8192]{1,0:T(8,128)S(1)}, u32[]{:S(2)}, u32[]{:S(2)}) %collective-permute-start.1) | collective-permute-done | bytes 524320 | tf_op jit(solution)/shard_map/ppermute | solution.py:12
  49.5 0.1 subtract_select_fusion
  49.5 8.1 %collective-permute-start.2 = (f32[16,8192]{1,0:T(8,128)S(1)}, f32[16,8192]{1,0:T(8,128)S(1)}, u32[]{:S(2)}, u32[]{:S(2)}) collective-permute-start(f32[16,8192]{1,0:T(8,128)S(1)} %subtract_select_fusion), channel_id=1, source_target_pairs={{0,4},{1,5},{2,6},{3,7},{4,0},{5,1},{6,2},{7,3},{8,12},{9,13},{10,... | collective-permute-start | bytes 1572872 | tf_op jit(solution)/shard_map/ppermute | solution.py:12
  57.6 22.1 %collective-permute-done.2 = f32[16,8192]{1,0:T(8,128)S(1)} collective-permute-done((f32[16,8192]{1,0:T(8,128)S(1)}, f32[16,8192]{1,0:T(8,128)S(1)}, u32[]{:S(2)}, u32[]{:S(2)}) %collective-permute-start.2) | collective-permute-done | bytes 524320 | tf_op jit(solution)/shard_map/ppermute | solution.py:12
  79.7 0.1 copy_bitcast_fusion.1
  79.7 29.8 %all_to_all.10 = f32[16,64,128]{2,0,1:T(8,128)S(1)} all-to-all(f32[16,64,128]{2,0,1:T(8,128)S(1)} %copy_bitcast_fusion.1), channel_id=1, replica_groups=mesh['wide'=64,'narrow'=8] {'wide'}, dimensions={1} | all-to-all | bytes 1048576 | tf_op jit(solution)/shard_map/all_to_all | solution.py:49
  109.5 0.8 convolution_bitcast_fusion
  110.3 1.1 copy.13
  111.4 5.7 %all-to-all-start.1 = ((f32[16,64,128]{2,0,1:T(8,128)}), f32[16,64,128]{2,0,1:T(8,128)S(1)}, u32[]{:S(2)}, u32[]{:S(2)}) async-start(f32[16,64,128]{2,0,1:T(8,128)} %copy.13), calls=%async_computation.1 | async-start | bytes 1048576 | tf_op jit(solution)/shard_map/all_to_all | solution.py:52
  117.1 0.0 copy-done
  117.2 17.7 %all-to-all-done.1 = f32[16,64,128]{2,0,1:T(8,128)S(1)} async-done(((f32[16,64,128]{2,0,1:T(8,128)}), f32[16,64,128]{2,0,1:T(8,128)S(1)}, u32[]{:S(2)}, u32[]{:S(2)}) %all-to-all-start.1) | async-done | bytes 524320 | tf_op jit(solution)/shard_map/all_to_all | solution.py:52
  134.9 2.6 %copy.14 = f32[16,64,128]{0,2,1:T(8,128)} copy(f32[16,64,128]{2,0,1:T(8,128)S(1)} %all-to-all-done.1) | data formatting | bytes 1048576 | tf_op jit(solution)/shard_map/all_to_all | solution.py:52
  137.5 5.0 %gather_fusion = f32[1024,16]{1,0:T(8,128)S(1)} fusion(f32[16,8192]{0,1:T(8,128)} %bitcast.30, s32[1024]{0:T(1024)S(1)} %fusion.45), kind=kCustom, calls=%fused_computation | custom fusion | bytes 135168 | tf_op jit(solution)/shard_map/jit(_take)/gather | solution.py:38
  142.4 0.2 fusion.1
  142.7 1.3 convolution_multiply_fusion
  143.9 0.8 copy.15
  144.7 97.0 %psum.7 = f32[16,16]{1,0:T(8,128)} all-reduce(f32[16,16]{1,0:T(8,128)S(1)} %convolution_multiply_fusion), channel_id=1, replica_groups=mesh['wide'=64,'narrow'=8] {'wide','narrow'}, use_global_device_ids=true, to_apply=%region_0.1 | all-reduce | flops 256 | bytes 2048 | tf_op jit(solution)/shard_map/psum | solution.py:74
  (2 shorter events, 0.0 us)
Async XLA Ops:
  4.1 12.3 %collective-permute-start = (f32[16,8192]{1,0:T(8,128)S(1)}, f32[16,8192]{1,0:T(8,128)S(1)}, u32[]{:S(2)}, u32[]{:S(2)}) collective-permute-start(f32[16,8192]{1,0:T(8,128)S(1)} %bitcast.34), channel_id=1, source_target_pairs={{0,1},{1,0},{2,3},{3,2},{4,5},{5,4},{6,7},{7,6},{8,9},{9,8},{10,11... | collective-permute-start | bytes 1572872 | tf_op jit(solution)/shard_map/ppermute | solution.py:12
  9.0 108.1 %copy-start = (s32[1024]{0:T(1024)S(1)}, s32[1024]{0:T(1024)}, u32[]{:S(2)}) copy-start(s32[1024]{0:T(1024)} %param.5) | copy-start | bytes 12292
  16.8 32.6 %collective-permute-start.1 = (f32[16,8192]{1,0:T(8,128)S(1)}, f32[16,8192]{1,0:T(8,128)S(1)}, u32[]{:S(2)}, u32[]{:S(2)}) collective-permute-start(f32[16,8192]{1,0:T(8,128)S(1)} %subtract_select_fusion.1), channel_id=1, source_target_pairs={{0,2},{1,3},{2,0},{3,1},{4,6},{5,7},{6,4},{7,5},{8,10},{9,11},{10,... | collective-permute-start | bytes 1572872 | tf_op jit(solution)/shard_map/ppermute | solution.py:12
  49.5 30.2 %collective-permute-start.2 = (f32[16,8192]{1,0:T(8,128)S(1)}, f32[16,8192]{1,0:T(8,128)S(1)}, u32[]{:S(2)}, u32[]{:S(2)}) collective-permute-start(f32[16,8192]{1,0:T(8,128)S(1)} %subtract_select_fusion), channel_id=1, source_target_pairs={{0,4},{1,5},{2,6},{3,7},{4,0},{5,1},{6,2},{7,3},{8,12},{9,13},{10,... | collective-permute-start | bytes 1572872 | tf_op jit(solution)/shard_map/ppermute | solution.py:12
  111.4 23.4 %all-to-all-start.1 = ((f32[16,64,128]{2,0,1:T(8,128)}), f32[16,64,128]{2,0,1:T(8,128)S(1)}, u32[]{:S(2)}, u32[]{:S(2)}) async-start(f32[16,64,128]{2,0,1:T(8,128)} %copy.13), calls=%async_computation.1 | async-start | bytes 1048576 | tf_op jit(solution)/shard_map/all_to_all | solution.py:52
where the time goes:
time: 242 us
  blocking collectives  127 us (52%)
  waiting for transfers between devices  69.9 us (29%)
  starting transfers between devices  28.6 us (12%)
  local copies, waits for them, and re-layouts  9.92 us (4%)
  matrix products  3.23 us (1%)
  other arithmetic  2.51 us (1%)
    psum x1, blocking collectives, shards(): sketch_gram = lax.psum(partial_gram, ('wide', 'narrow'))  97 us
    ppermute x3, waiting for transfers between devices, from_partner(): return lax.ppermute(value, axis, pairs)  52.3 us
    all_to_all x1, blocking collectives, wide_section(): lax.all_to_all(blocked, 'wide', split_axis=1, concat_axis=1, tiled=True)  29.8 us
    ppermute x3, starting transfers between devices, from_partner(): return lax.ppermute(value, axis, pairs)  22.8 us
    all_to_all x1, waiting for transfers between devices, wide_section(): lax.all_to_all(mixed_rows, 'wide', split_axis=1, concat_axis=1, tiled=True)  17.7 us
    all_to_all x1, starting transfers between devices, wide_section(): lax.all_to_all(mixed_rows, 'wide', split_axis=1, concat_axis=1, tiled=True)  5.73 us
    gather x1, local copies, waits for them, and re-layouts, pick_samples(): return jnp.take(values, local_rows, axis=1)  4.99 us
  transfers between devices with their start and end apart: 4, of which 4 were waited for; matrix products, arithmetic and copies ran while one was open for 0% of the time, Pallas kernels for 0%

commit v1 on v0

v1 whole, which is shorter than its diff:
```python
import functools
import math

import jax
import jax.numpy as jnp
from jax import lax
from jax.experimental import pallas as pl
from jax.experimental.pallas import tpu as pltpu
from jax.sharding import PartitionSpec as P

MESH = pl.DeviceIdType.MESH
F32, BF16 = jnp.float32, jnp.bfloat16


def parity_sign(a, b, bits):
    common = a & b
    parity = jnp.zeros_like(common)
    for bit in range(bits):
        parity = parity ^ (common >> bit & 1)
    return (1 - 2 * parity).astype(F32)


def butterfly(tiles):
    tiles, step = list(tiles), 1
    while step < len(tiles):
        for i in range(len(tiles)):
            if not i & step:
                a, b = tiles[i], tiles[i + step]
                tiles[i], tiles[i + step] = a + b, a - b
        step *= 2
    return tiles


def parts(value, axis):
    high = value.astype(BF16)
    low = (value - high.astype(F32)).astype(BF16)
    return jnp.concatenate([high, low], axis=axis)


def kernel(
    nw, nz, scale, gram_scale,
    x_ref, sign_ref, rows_ref, sketch_ref, gram_ref,
    own, tiles, pick_own, pick_tiles, mixed, slabs, pick_z, picks,
    chosen, back, turn, ret, rec, gram_own, gram_w, gram_zown, gram_z,
    sem_w, sem_z, sem_p, sem_b, sem_g, sem_c,
):
    w, z = lax.axis_index("wide"), lax.axis_index("narrow")
    barrier = pltpu.get_barrier_semaphore()

    def each_wide(body):
        def step(i, carry):
            body(lax.rem(w + i, nw))
            return carry

        lax.fori_loop(1, nw, step, 0)

    def each_narrow(body):
        for i in range(1, nz):
            body(lax.rem(z + i, nz))

    each_wide(lambda p: pl.semaphore_signal(barrier, inc=1, device_id=(p, z), device_id_type=MESH))
    each_narrow(lambda p: pl.semaphore_signal(barrier, inc=1, device_id=(w, p), device_id_type=MESH))

    def to_wide(src, dst, sems, p):
        pltpu.make_async_remote_copy(
            src, dst, sems.at[0], sems.at[1], device_id=(p, z), device_id_type=MESH
        ).start()

    def to_narrow(src, dst, sems, p):
        pltpu.make_async_remote_copy(
            src, dst, sems.at[0], sems.at[1], device_id=(w, p), device_id_type=MESH
        ).start()

    def await_all(ref, sem):
        pltpu.make_async_copy(ref, ref, sem).wait()

    lane_i = lax.broadcasted_iota(jnp.int32, (128, 128), 1)
    row_i = lax.broadcasted_iota(jnp.int32, (128, 128), 0)
    lane_table = parity_sign(lane_i, row_i, 7).astype(BF16)
    lane_table = jnp.concatenate([lane_table, lane_table], axis=0)
    wide_table = jnp.where(lane_i // nw == row_i // nw, parity_sign(lane_i, row_i, 6), 0.0).astype(BF16)
    wide_table = jnp.concatenate([wide_table, wide_table], axis=0)

    offsets = rows_ref[...].astype(F32)
    for t in range(8):
        pick_own[t] = offsets[t : t + 1]

    def local(h):
        cols = slice(8 * h, 8 * h + 8)
        for g in range(8):
            part = []
            for i in range(8):
                t = g * 8 + i
                sign = sign_ref[t : t + 1, :].astype(F32)
                part.append(x_ref[cols, 128 * t : 128 * t + 128] * sign)
            for i, tile in enumerate(butterfly(part)):
                own[h, pl.ds(8 * (g * 8 + i), 8), :] = tile
        for g in range(8):
            part = butterfly([own[h, pl.ds(8 * (i * 8 + g), 8), :] for i in range(8)])
            value = jnp.dot(
                parts(jnp.concatenate(part, axis=0), 1), lane_table, preferred_element_type=F32
            )
            for i in range(8):
                own[h, pl.ds(8 * (i * 8 + g), 8), :] = value[8 * i : 8 * i + 8]

    def send_half(h):
        mine = pl.ds(pl.multiple_of(w * 8, 8), 8)

        def send(p):
            to_wide(own.at[h, pl.ds(pl.multiple_of(p * 8, 8), 8)], tiles.at[h, mine], sem_w.at[h], p)

        each_wide(send)
        tiles[h, mine, :] = own[h, mine, :]

    local(0)
    pl.semaphore_wait(barrier, nw - 1 + nz - 1)
    each_wide(lambda p: to_wide(pick_own.at[lax.div(p, 8)], pick_tiles.at[w], sem_p, p))
    pick_tiles[w] = pick_own[lax.div(w, 8)]
    send_half(0)
    local(1)
    send_half(1)

    await_all(pick_tiles.at[pl.ds(0, nw - 1)], sem_p.at[1])
    gathered = pick_tiles[...].reshape(nw, 128).astype(BF16)
    gathered = jnp.concatenate([gathered, gathered], axis=0)
    first = lax.rem(w, 8) * 16
    choose = (lane_i[:16] == row_i[:16] + first).astype(BF16)
    by_run = lax.dot_general(
        choose, gathered, (((1,), (1,)), ((), ())), preferred_element_type=F32
    )
    for k in range(8):
        pick_z[k] = by_run[2 * k : 2 * k + 2]
    each_narrow(lambda p: to_narrow(pick_z.at[p], picks.at[z], sem_c, p))
    picks[z] = pick_z[z]

    for h in range(2):
        await_all(tiles.at[h, pl.ds(0, 8 * (nw - 1))], sem_w.at[h, 1])
        for p in range(4):
            value = jnp.concatenate(
                [tiles[h, pl.ds(4 * c + p, nw, stride=8), :] for c in range(2)], axis=0
            )
            value = jnp.dot(parts(value.T, 1), wide_table, preferred_element_type=F32)
            for k in range(8):
                mixed[h, k, 16 * p : 16 * p + 16, :] = value[16 * k : 16 * k + 16]
        each_narrow(lambda p: to_narrow(mixed.at[h, p], slabs.at[h, z], sem_z.at[h], p))
        slabs[h, z] = mixed[h, z]

    await_all(picks.at[pl.ds(0, nz - 1)], sem_c.at[1])
    place = lax.broadcasted_iota(jnp.int32, (8, 128), 0).astype(F32)
    for h in range(2):
        await_all(slabs.at[h, pl.ds(0, nz - 1)], sem_z.at[h, 1])
        for k in range(2):
            masks = [picks[d, k : k + 1, :] == place for d in range(nz)]
            for p in range(4):
                at = 16 * p + 8 * k
                out = butterfly([slabs[h, s, at : at + 8, :] for s in range(nz)])
                for d in range(nz):
                    one = jnp.sum(jnp.where(masks[d], out[d], 0.0), axis=0, keepdims=True)
                    row = 8 * k + 4 * h + p
                    chosen[d, row : row + 1, :] = one * scale

    each_narrow(lambda p: to_narrow(chosen.at[p], back.at[z], sem_b, p))
    back[z] = chosen[z]

    lane = lane_i[:8]
    sub = row_i[:8]
    terms = []
    for d in range(nz):
        one, two = chosen[d, 0:8, :], chosen[d, 8:16, :]
        even = jnp.where(lane < 64, one, pltpu.roll(two, 64, 1))
        odd = jnp.where(lane < 64, pltpu.roll(one, 64, 1), two)
        top = jnp.where(sub < 4, even, pltpu.roll(odd, 4, 0))
        low = jnp.where(sub < 4, pltpu.roll(even, 4, 0), odd)
        terms.append(jnp.concatenate([top, low], axis=0))
    columns = jnp.concatenate(terms, axis=1)
    wide_gram = lax.dot_general(
        columns, jnp.concatenate([columns] * 8, axis=0), (((1,), (1,)), ((), ())),
        precision=lax.Precision.HIGHEST, preferred_element_type=F32,
    )
    diagonal = lane // 16 == sub
    for a in range(2):
        gram_own[0, a : a + 1, :] = jnp.sum(
            jnp.where(diagonal, wide_gram[8 * a : 8 * a + 8], 0.0), axis=0, keepdims=True
        )
    each_wide(lambda p: to_wide(gram_own.at[0], gram_w.at[w], sem_g.at[0], p))
    gram_w[w] = gram_own[0]

    await_all(back.at[pl.ds(0, nz - 1)], sem_b.at[1])
    for s in range(nz):
        for k in range(2):
            turn[pl.ds(2 * s + k, 8, stride=16), :] = back[s, 8 * k : 8 * k + 8, :]
    turned = turn[...].T
    ret[:, 0, :] = turned[:nw]
    ret[:, 1, :] = turned[nw:]
    each_wide(lambda p: to_wide(ret.at[p], rec.at[w], sem_p.at[pl.ds(2, 2)], p))
    rec[w] = ret[w]

    await_all(gram_w.at[pl.ds(0, nw - 1)], sem_g.at[0, 1])
    gram_zown[0] = jnp.sum(gram_w[...], axis=0)
    each_narrow(lambda p: to_narrow(gram_zown.at[0], gram_z.at[z], sem_g.at[1], p))
    gram_z[z] = gram_zown[0]

    await_all(rec.at[pl.ds(0, nw - 1)], sem_p.at[3])
    group = lane // 16
    for t in range(8):
        for c in range(2):
            value = rec[8 * t : 8 * t + 8, c, :]
            for bit in (1, 2, 4):
                down = pltpu.roll(pltpu.roll(value, 8 - bit, 0), 16 * bit, 1)
                up = pltpu.roll(pltpu.roll(value, bit, 0), 128 - 16 * bit, 1)
                upper, right = (sub & bit) != 0, (group & bit) != 0
                value = jnp.where(upper == right, value, jnp.where(right, down, up))
            for e in range(2):
                sketch_ref[8 * e + 4 * c : 8 * e + 4 * c + 4, 128 * t : 128 * t + 128] = value[4 * e : 4 * e + 4]

    await_all(gram_z.at[pl.ds(0, nz - 1)], sem_g.at[1, 1])
    gram_ref[...] = jnp.sum(gram_z[...], axis=0) * gram_scale

    for h in range(2):
        await_all(tiles.at[h, pl.ds(0, 8 * (nw - 1))], sem_w.at[h, 0])
        await_all(slabs.at[h, pl.ds(0, nz - 1)], sem_z.at[h, 0])
    await_all(pick_tiles.at[pl.ds(0, nw - 1)], sem_p.at[0])
    await_all(rec.at[pl.ds(0, nw - 1)], sem_p.at[2])
    await_all(picks.at[pl.ds(0, nz - 1)], sem_c.at[0])
    await_all(back.at[pl.ds(0, nz - 1)], sem_b.at[0])
    await_all(gram_w.at[pl.ds(0, nw - 1)], sem_g.at[0, 0])
    await_all(gram_z.at[pl.ds(0, nz - 1)], sem_g.at[1, 0])


def solution(mesh):
    nw, nz = mesh.shape["wide"], mesh.shape["narrow"]

    def shards(matrix_slab, row_signs, sample_rows):
        cols, rows = matrix_slab.shape
        samples = sample_rows.shape[0]
        dma = pltpu.SemaphoreType.DMA
        sketch, gram = pl.pallas_call(
            functools.partial(
                kernel, nw, nz, 1.0 / math.sqrt(rows * nw * nz), 1.0 / (samples * nw * nz)
            ),
            out_shape=(
                jax.ShapeDtypeStruct((cols, samples), F32),
                jax.ShapeDtypeStruct((2, 128), F32),
            ),
            in_specs=[pl.BlockSpec(memory_space=pltpu.VMEM)] * 3,
            out_specs=[pl.BlockSpec(memory_space=pltpu.VMEM)] * 2,
            scratch_shapes=[
                pltpu.VMEM((2, 8 * nw, 128), F32),
                pltpu.VMEM((2, 8 * nw, 128), F32),
                pltpu.VMEM((8, 1, 128), F32),
                pltpu.VMEM((nw, 1, 128), F32),
                pltpu.VMEM((2, nz, 64, 128), F32),
                pltpu.VMEM((2, nz, 64, 128), F32),
                pltpu.VMEM((nz, 2, 128), F32),
                pltpu.VMEM((nz, 2, 128), F32),
                pltpu.VMEM((nz, 16, 128), F32),
                pltpu.VMEM((nz, 16, 128), F32),
                pltpu.VMEM((128, 128), F32),
                pltpu.VMEM((nw, 2, 128), F32),
                pltpu.VMEM((nw, 2, 128), F32),
                pltpu.VMEM((1, 2, 128), F32),
                pltpu.VMEM((nw, 2, 128), F32),
                pltpu.VMEM((1, 2, 128), F32),
                pltpu.VMEM((nz, 2, 128), F32),
                dma((2, 2)),
                dma((2, 2)),
                dma((4,)),
                dma((2,)),
                dma((2, 2)),
                dma((2,)),
            ],
            compiler_params=pltpu.CompilerParams(
                collective_id=0, has_side_effects=True, vmem_limit_bytes=32 << 20
            ),
            name="hadamard_sketch",
        )(matrix_slab, row_signs.reshape(-1, 128), sample_rows.reshape(-1, 128))
        return sketch, gram.reshape(cols, cols)

    in_specs = (P(None, ("wide", "narrow")), P(("wide", "narrow")), P(("wide", "narrow")))
    out_specs = (P(None, ("wide", "narrow")), P())
    return jax.shard_map(shards, mesh=mesh, in_specs=in_specs, out_specs=out_specs, check_vma=False)
```

time: 242 us -> 59.1 us (0.24)
  blocking collectives: 127 us -> 0 us
  waiting for transfers between devices: 69.9 us -> 0 us
  Pallas kernels: 0 us -> 54.4 us
  starting transfers between devices: 28.6 us -> 0 us
  local copies, waits for them, and re-layouts: 9.92 us -> 3.79 us
  matrix products: 3.23 us -> 0 us
  other arithmetic: 2.51 us -> 0 us
    psum x1 -> x0, blocking collectives: 97 us -> none  [shards(): sketch_gram = lax.psum(partial_gram, ('wide', 'narrow'))]
    pallas_call x0 -> x1, Pallas kernels: none -> 54.4 us  [shards(): pl.pallas_call(functools.partial(kernel, nw, nz, 1.0 / math.sqrt(rows * n...]
    ppermute x3 -> x0, waiting for transfers between devices: 52.3 us -> none  [from_partner(): return lax.ppermute(value, axis, pairs)]
    all_to_all x1 -> x0, blocking collectives: 29.8 us -> none  [wide_section(): lax.all_to_all(blocked, 'wide', split_axis=1, concat_axis=1, tiled=True)]
    ppermute x3 -> x0, starting transfers between devices: 22.8 us -> none  [from_partner(): return lax.ppermute(value, axis, pairs)]
    all_to_all x1 -> x0, waiting for transfers between devices: 17.7 us -> none  [wide_section(): lax.all_to_all(mixed_rows, 'wide', split_axis=1, concat_axis=1, tiled=True)]
    all_to_all x1 -> x0, starting transfers between devices: 5.73 us -> none  [wide_section(): lax.all_to_all(mixed_rows, 'wide', split_axis=1, concat_axis=1, tiled=True)]
    gather x1 -> x0, local copies, waits for them, and re-layouts: 4.99 us -> none  [pick_samples(): return jnp.take(values, local_rows, axis=1)]
  transfers between devices with their start and end apart: 4 -> 0, of which waited for: 4 -> 0; matrix products, arithmetic and copies ran while one was open for 0% -> 0% of each run, Pallas kernels for 0% -> 0%
where the time goes in v1:
time: 59.1 us; the launch traced here: 58.8 us
  Pallas kernels  54.4 us (92%)
  local copies, waits for them, and re-layouts  3.79 us (6%)
  between operations  0.65 us (1%)
    pallas_call x1, Pallas kernels, shards(): pl.pallas_call(functools.partial(kernel, nw, nz, 1.0 / math.sqrt(rows * n...  54.4 us
    unnamed x7, local copies, waits for them, and re-layouts  3.11 us

profile of v1, /device:TPU:1, one launch (start us, length us, event | category | flops | bytes accessed | tf_op | source)
XLA Modules:
  0.0 58.8 jit_solution(1529485235168272435)
XLA Ops:
  0.6 0.0 copy-start
  0.6 1.0 %copy-done = f32[16,8192]{1,0:T(8,128)S(1)} copy-done((f32[16,8192]{1,0:T(8,128)S(1)}, f32[16,8192]{1,0:T(8,128)}, u32[]{:S(2)}) %copy-start) | copy-done | bytes 524312
  1.7 0.0 copy-start.1
  1.7 0.8 %copy-done.1 = s32[8192]{0:T(1024)S(1)} copy-done((s32[8192]{0:T(1024)S(1)}, s32[8192]{0:T(1024)}, u32[]{:S(2)}) %copy-start.1) | copy-done | bytes 32792
  2.4 0.0 copy-start.2
  2.4 0.7 %copy-done.2 = s32[1024]{0:T(1024)S(1)} copy-done((s32[1024]{0:T(1024)S(1)}, s32[1024]{0:T(1024)}, u32[]{:S(2)}) %copy-start.2) | copy-done | bytes 4120
  3.1 54.4 %hadamard_sketch.1 = (f32[16,1024]{1,0:T(8,128)S(1)}, f32[2,128]{1,0:T(2,128)S(1)}) custom-call(f32[16,8192]{1,0:T(8,128)S(1)} %copy-done, s32[64,128]{1,0:T(8,128)S(1)} %bitcast.2, s32[8,128]{1,0:T(8,128)S(1)} %bitcast.3), custom_call_target="tpu_custom_call" | custom-call | tf_op jit(solution)/shard_map/hadamard_sketch/pallas_call | solution.py:237
  57.5 0.7 %reshape.15 = f32[16,16]{1,0:T(8,128)} reshape(f32[2,128]{1,0:T(2,128)S(1)} %get-tuple-element.5) | data formatting | bytes 2048 | tf_op jit(solution)/shard_map/reshape | solution.py:277
  58.2 0.6 %copy.6 = f32[16,1024]{1,0:T(8,128)} copy(f32[16,1024]{1,0:T(8,128)S(1)} %get-tuple-element.8) | data formatting | bytes 131072
Async XLA Ops:
  0.6 1.0 %copy-start = (f32[16,8192]{1,0:T(8,128)S(1)}, f32[16,8192]{1,0:T(8,128)}, u32[]{:S(2)}) copy-start(f32[16,8192]{1,0:T(8,128)} %x_ref.1) | copy-start | bytes 1572868
  1.7 0.8 %copy-start.1 = (s32[8192]{0:T(1024)S(1)}, s32[8192]{0:T(1024)}, u32[]{:S(2)}) copy-start(s32[8192]{0:T(1024)} %param.4) | copy-start | bytes 98308
  2.4 0.7 %copy-start.2 = (s32[1024]{0:T(1024)S(1)}, s32[1024]{0:T(1024)}, u32[]{:S(2)}) copy-start(s32[1024]{0:T(1024)} %param.5) | copy-start | bytes 12292

commit v2 on v1

--- a/solution.py
+++ b/solution.py
@@ -39,27 +39,40 @@
 
 def kernel(
     nw, nz, scale, gram_scale,
-    x_ref, sign_ref, rows_ref, sketch_ref, gram_ref,
+    x_hbm, sign_hbm, rows_hbm, sketch_ref, gram_ref, x_ref, sign_ref, rows_ref,
     own, tiles, pick_own, pick_tiles, mixed, slabs, pick_z, picks,
     chosen, back, turn, ret, rec, gram_own, gram_w, gram_zown, gram_z,
-    sem_w, sem_z, sem_p, sem_b, sem_g, sem_c,
+    sem_in, sem_w, sem_z, sem_p, sem_b, sem_g, sem_c,
 ):
     w, z = lax.axis_index("wide"), lax.axis_index("narrow")
     barrier = pltpu.get_barrier_semaphore()
 
+    inputs = [
+        pltpu.make_async_copy(x_hbm.at[pl.ds(8 * h, 8)], x_ref.at[h], sem_in.at[h]) for h in range(2)
+    ]
+    inputs.append(pltpu.make_async_copy(sign_hbm, sign_ref, sem_in.at[2]))
+    inputs.append(pltpu.make_async_copy(rows_hbm, rows_ref, sem_in.at[3]))
+    for i in (0, 2, 1, 3):
+        inputs[i].start()
+
+    y, j = lax.div(w, 8), lax.rem(w, 8)
+
     def each_wide(body):
         def step(i, carry):
-            body(lax.rem(w + i, nw))
+            k = lax.div(i, 8)
+            half = lax.div(k + 1, 2)
+            along = jnp.where(lax.rem(k, 2) == 1, 4 - half, 4 + half)
+            body(lax.rem(y + along, 8) * 8 + lax.rem(j + 1 + lax.rem(i, 8), 8))
             return carry
 
-        lax.fori_loop(1, nw, step, 0)
+        lax.fori_loop(0, nw - 1, step, 0)
 
     def each_narrow(body):
-        for i in range(1, nz):
+        for i in (4, 3, 5, 2, 6, 1, 7):
             body(lax.rem(z + i, nz))
 
+    each_narrow(lambda p: pl.semaphore_signal(barrier, inc=1, device_id=(w, p), device_id_type=MESH))
     each_wide(lambda p: pl.semaphore_signal(barrier, inc=1, device_id=(p, z), device_id_type=MESH))
-    each_narrow(lambda p: pl.semaphore_signal(barrier, inc=1, device_id=(w, p), device_id_type=MESH))
 
     def to_wide(src, dst, sems, p):
         pltpu.make_async_remote_copy(
@@ -81,18 +94,13 @@
     wide_table = jnp.where(lane_i // nw == row_i // nw, parity_sign(lane_i, row_i, 6), 0.0).astype(BF16)
     wide_table = jnp.concatenate([wide_table, wide_table], axis=0)
 
-    offsets = rows_ref[...].astype(F32)
-    for t in range(8):
-        pick_own[t] = offsets[t : t + 1]
-
     def local(h):
-        cols = slice(8 * h, 8 * h + 8)
         for g in range(8):
             part = []
             for i in range(8):
                 t = g * 8 + i
                 sign = sign_ref[t : t + 1, :].astype(F32)
-                part.append(x_ref[cols, 128 * t : 128 * t + 128] * sign)
+                part.append(x_ref[h, :, 128 * t : 128 * t + 128] * sign)
             for i, tile in enumerate(butterfly(part)):
                 own[h, pl.ds(8 * (g * 8 + i), 8), :] = tile
         for g in range(8):
@@ -112,13 +120,33 @@
         each_wide(send)
         tiles[h, mine, :] = own[h, mine, :]
 
+    inputs[2].wait()
+    inputs[0].wait()
     local(0)
     pl.semaphore_wait(barrier, nw - 1 + nz - 1)
+    send_half(0)
+    inputs[1].wait()
+    local(1)
+    send_half(1)
+
+    inputs[3].wait()
+    offsets = rows_ref[...].astype(F32)
+    for t in range(8):
+        pick_own[t] = offsets[t : t + 1]
     each_wide(lambda p: to_wide(pick_own.at[lax.div(p, 8)], pick_tiles.at[w], sem_p, p))
     pick_tiles[w] = pick_own[lax.div(w, 8)]
-    send_half(0)
-    local(1)
-    send_half(1)
+
+    for h in range(2):
+        await_all(tiles.at[h, pl.ds(0, 8 * (nw - 1))], sem_w.at[h, 1])
+        for p in range(4):
+            value = jnp.concatenate(
+                [tiles[h, pl.ds(4 * c + p, nw, stride=8), :] for c in range(2)], axis=0
+            )
+            value = jnp.dot(parts(value.T, 1), wide_table, preferred_element_type=F32)
+            for k in range(8):
+                mixed[h, k, 16 * p : 16 * p + 16, :] = value[16 * k : 16 * k + 16]
+        each_narrow(lambda p: to_narrow(mixed.at[h, p], slabs.at[h, z], sem_z.at[h], p))
+        slabs[h, z] = mixed[h, z]
 
     await_all(pick_tiles.at[pl.ds(0, nw - 1)], sem_p.at[1])
     gathered = pick_tiles[...].reshape(nw, 128).astype(BF16)
@@ -132,18 +160,6 @@
         pick_z[k] = by_run[2 * k : 2 * k + 2]
     each_narrow(lambda p: to_narrow(pick_z.at[p], picks.at[z], sem_c, p))
     picks[z] = pick_z[z]
-
-    for h in range(2):
-        await_all(tiles.at[h, pl.ds(0, 8 * (nw - 1))], sem_w.at[h, 1])
-        for p in range(4):
-            value = jnp.concatenate(
-                [tiles[h, pl.ds(4 * c + p, nw, stride=8), :] for c in range(2)], axis=0
-            )
-            value = jnp.dot(parts(value.T, 1), wide_table, preferred_element_type=F32)
-            for k in range(8):
-                mixed[h, k, 16 * p : 16 * p + 16, :] = value[16 * k : 16 * k + 16]
-        each_narrow(lambda p: to_narrow(mixed.at[h, p], slabs.at[h, z], sem_z.at[h], p))
-        slabs[h, z] = mixed[h, z]
 
     await_all(picks.at[pl.ds(0, nz - 1)], sem_c.at[1])
     place = lax.broadcasted_iota(jnp.int32, (8, 128), 0).astype(F32)
@@ -242,9 +258,12 @@
                 jax.ShapeDtypeStruct((cols, samples), F32),
                 jax.ShapeDtypeStruct((2, 128), F32),
             ),
-            in_specs=[pl.BlockSpec(memory_space=pltpu.VMEM)] * 3,
+            in_specs=[pl.BlockSpec(memory_space=pl.ANY)] * 3,
             out_specs=[pl.BlockSpec(memory_space=pltpu.VMEM)] * 2,
             scratch_shapes=[
+                pltpu.VMEM((2, 8, 8192), F32),
+                pltpu.VMEM((64, 128), jnp.int32),
+                pltpu.VMEM((8, 128), jnp.int32),
                 pltpu.VMEM((2, 8 * nw, 128), F32),
                 pltpu.VMEM((2, 8 * nw, 128), F32),
                 pltpu.VMEM((8, 1, 128), F32),
@@ -262,6 +281,7 @@
                 pltpu.VMEM((nw, 2, 128), F32),
                 pltpu.VMEM((1, 2, 128), F32),
                 pltpu.VMEM((nz, 2, 128), F32),
+                dma((4,)),
                 dma((2, 2)),
                 dma((2, 2)),
                 dma((4,)),
@@ -269,9 +289,7 @@
                 dma((2, 2)),
                 dma((2,)),
             ],
-            compiler_params=pltpu.CompilerParams(
-                collective_id=0, has_side_effects=True, vmem_limit_bytes=32 << 20
-            ),
+            compiler_params=pltpu.CompilerParams(collective_id=0, has_side_effects=True),
             name="hadamard_sketch",
         )(matrix_slab, row_signs.reshape(-1, 128), sample_rows.reshape(-1, 128))
         return sketch, gram.reshape(cols, cols)

time: 59.1 us -> 57 us (0.964)
  Pallas kernels: 54.4 us -> 53.4 us
  local copies, waits for them, and re-layouts: 3.79 us -> 2.81 us
    pallas_call x1, Pallas kernels: 54.4 us -> 53.4 us  [shards(): pl.pallas_call(functools.partial(kernel, nw, nz, 1.0 / math.sqrt(rows * n...]
    unnamed x7 -> x3, local copies, waits for them, and re-layouts: 3.11 us -> 2.13 us
where the time goes in v2:
time: 57 us; the launch traced here: 56.8 us
  Pallas kernels  53.4 us (94%)
  local copies, waits for them, and re-layouts  2.81 us (5%)
  between operations  0.65 us (1%)
    pallas_call x1, Pallas kernels, shards(): pl.pallas_call(functools.partial(kernel, nw, nz, 1.0 / math.sqrt(rows * n...  53.4 us
    unnamed x3, local copies, waits for them, and re-layouts  2.13 us

profile of v2, /device:TPU:1, one launch (start us, length us, event | category | flops | bytes accessed | tf_op | source)
XLA Modules:
  0.0 56.8 jit_solution(16950922397820895157)
XLA Ops:
  0.6 53.4 %hadamard_sketch.1 = (f32[16,1024]{1,0:T(8,128)}, f32[2,128]{1,0:T(2,128)}) custom-call(f32[16,8192]{1,0:T(8,128)} %x_hbm.1, s32[64,128]{1,0:T(8,128)} %bitcast.2, s32[8,128]{1,0:T(8,128)} %bitcast.3), custom_call_target="tpu_custom_call" | custom-call | tf_op jit(solution)/shard_map/hadamard_sketch/pallas_call | solution.py:253
  54.0 0.0 copy-start
  54.0 0.7 %copy-done = f32[2,128]{1,0:T(2,128)S(1)} copy-done((f32[2,128]{1,0:T(2,128)S(1)}, f32[2,128]{1,0:T(2,128)}, u32[]{:S(2)}) %copy-start) | copy-done | bytes 1048
  54.7 0.7 %reshape.15 = f32[16,16]{1,0:T(8,128)} reshape(f32[2,128]{1,0:T(2,128)S(1)} %copy-done) | data formatting | bytes 2048 | tf_op jit(solution)/shard_map/reshape | solution.py:295
  55.4 1.5 %copy.6 = f32[16,1024]{1,0:T(8,128)} copy(f32[16,1024]{1,0:T(8,128)} %get-tuple-element.8) | data formatting | bytes 131072
Async XLA Ops:
  54.0 0.7 %copy-start = (f32[2,128]{1,0:T(2,128)S(1)}, f32[2,128]{1,0:T(2,128)}, u32[]{:S(2)}) copy-start(f32[2,128]{1,0:T(2,128)} %get-tuple-element.5) | copy-start | bytes 3076

commit v3 on v2

--- a/solution.py
+++ b/solution.py
@@ -44,7 +44,12 @@
     chosen, back, turn, ret, rec, gram_own, gram_w, gram_zown, gram_z,
     sem_in, sem_w, sem_z, sem_p, sem_b, sem_g, sem_c,
 ):
-    w, z = lax.axis_index("wide"), lax.axis_index("narrow")
+    wide, narrow = lax.axis_index("wide"), lax.axis_index("narrow")
+    w, z = lax.div(wide, 8) * 8 + narrow, lax.rem(wide, 8)
+
+    def device(group, member):
+        return (lax.div(group, 8) * 8 + member, lax.rem(group, 8))
+
     barrier = pltpu.get_barrier_semaphore()
 
     inputs = [
@@ -71,17 +76,17 @@
         for i in (4, 3, 5, 2, 6, 1, 7):
             body(lax.rem(z + i, nz))
 
-    each_narrow(lambda p: pl.semaphore_signal(barrier, inc=1, device_id=(w, p), device_id_type=MESH))
-    each_wide(lambda p: pl.semaphore_signal(barrier, inc=1, device_id=(p, z), device_id_type=MESH))
+    each_narrow(lambda p: pl.semaphore_signal(barrier, inc=1, device_id=device(w, p), device_id_type=MESH))
+    each_wide(lambda p: pl.semaphore_signal(barrier, inc=1, device_id=device(p, z), device_id_type=MESH))
 
     def to_wide(src, dst, sems, p):
         pltpu.make_async_remote_copy(
-            src, dst, sems.at[0], sems.at[1], device_id=(p, z), device_id_type=MESH
+            src, dst, sems.at[0], sems.at[1], device_id=device(p, z), device_id_type=MESH
         ).start()
 
     def to_narrow(src, dst, sems, p):
         pltpu.make_async_remote_copy(
-            src, dst, sems.at[0], sems.at[1], device_id=(w, p), device_id_type=MESH
+            src, dst, sems.at[0], sems.at[1], device_id=device(w, p), device_id_type=MESH
         ).start()
 
     def await_all(ref, sem):

time: 57 us -> 54.1 us (0.949)
  Pallas kernels: 53.4 us -> 50.5 us
    pallas_call x1, Pallas kernels: 53.4 us -> 50.5 us  [shards(): pl.pallas_call(functools.partial(kernel, nw, nz, 1.0 / math.sqrt(rows * n...]
where the time goes in v3:
time: 54.1 us; the launch traced here: 54 us
  Pallas kernels  50.5 us (93%)
  local copies, waits for them, and re-layouts  2.81 us (5%)
  between operations  0.65 us (1%)
    pallas_call x1, Pallas kernels, shards(): pl.pallas_call(functools.partial(kernel, nw, nz, 1.0 / math.sqrt(rows * n...  50.5 us
    unnamed x3, local copies, waits for them, and re-layouts  2.13 us

profile of v3, /device:TPU:1, one launch (start us, length us, event | category | flops | bytes accessed | tf_op | source)
XLA Modules:
  0.0 54.0 jit_solution(428221077105679460)
XLA Ops:
  0.6 50.5 %hadamard_sketch.1 = (f32[16,1024]{1,0:T(8,128)}, f32[2,128]{1,0:T(2,128)}) custom-call(f32[16,8192]{1,0:T(8,128)} %x_hbm.1, s32[64,128]{1,0:T(8,128)} %bitcast.2, s32[8,128]{1,0:T(8,128)} %bitcast.3), custom_call_target="tpu_custom_call" | custom-call | tf_op jit(solution)/shard_map/hadamard_sketch/pallas_call | solution.py:258
  51.1 0.0 copy-start
  51.2 0.7 %copy-done = f32[2,128]{1,0:T(2,128)S(1)} copy-done((f32[2,128]{1,0:T(2,128)S(1)}, f32[2,128]{1,0:T(2,128)}, u32[]{:S(2)}) %copy-start) | copy-done | bytes 1048
  51.8 0.7 %reshape.15 = f32[16,16]{1,0:T(8,128)} reshape(f32[2,128]{1,0:T(2,128)S(1)} %copy-done) | data formatting | bytes 2048 | tf_op jit(solution)/shard_map/reshape | solution.py:300
  52.5 1.5 %copy.6 = f32[16,1024]{1,0:T(8,128)} copy(f32[16,1024]{1,0:T(8,128)} %get-tuple-element.8) | data formatting | bytes 131072
Async XLA Ops:
  51.1 0.7 %copy-start = (f32[2,128]{1,0:T(2,128)S(1)}, f32[2,128]{1,0:T(2,128)}, u32[]{:S(2)}) copy-start(f32[2,128]{1,0:T(2,128)} %get-tuple-element.5) | copy-start | bytes 3076

commit v4 on v3

--- a/solution.py
+++ b/solution.py
@@ -39,7 +39,7 @@
 
 def kernel(
     nw, nz, scale, gram_scale,
-    x_hbm, sign_hbm, rows_hbm, sketch_ref, gram_ref, x_ref, sign_ref, rows_ref,
+    x_hbm, sign_hbm, rows_hbm, samples_ref, gram_ref, x_ref, sign_ref, rows_ref,
     own, tiles, pick_own, pick_tiles, mixed, slabs, pick_z, picks,
     chosen, back, turn, ret, rec, gram_own, gram_w, gram_zown, gram_z,
     sem_in, sem_w, sem_z, sem_p, sem_b, sem_g, sem_c,
@@ -96,9 +96,6 @@
     row_i = lax.broadcasted_iota(jnp.int32, (128, 128), 0)
     lane_table = parity_sign(lane_i, row_i, 7).astype(BF16)
     lane_table = jnp.concatenate([lane_table, lane_table], axis=0)
-    wide_table = jnp.where(lane_i // nw == row_i // nw, parity_sign(lane_i, row_i, 6), 0.0).astype(BF16)
-    wide_table = jnp.concatenate([wide_table, wide_table], axis=0)
-
     def local(h):
         for g in range(8):
             part = []
@@ -134,6 +131,9 @@
     local(1)
     send_half(1)
 
+    wide_table = jnp.where(lane_i // nw == row_i // nw, parity_sign(lane_i, row_i, 6), 0.0).astype(BF16)
+    wide_table = jnp.concatenate([wide_table, wide_table], axis=0)
+
     inputs[3].wait()
     offsets = rows_ref[...].astype(F32)
     for t in range(8):
@@ -194,9 +194,12 @@
         low = jnp.where(sub < 4, pltpu.roll(even, 4, 0), odd)
         terms.append(jnp.concatenate([top, low], axis=0))
     columns = jnp.concatenate(terms, axis=1)
+    high = columns.astype(BF16)
+    low = (columns - high.astype(F32)).astype(BF16)
+    repeated = jnp.concatenate([jnp.concatenate([high, low, high], axis=1)] * 8, axis=0)
     wide_gram = lax.dot_general(
-        columns, jnp.concatenate([columns] * 8, axis=0), (((1,), (1,)), ((), ())),
-        precision=lax.Precision.HIGHEST, preferred_element_type=F32,
+        jnp.concatenate([high, high, low], axis=1), repeated, (((1,), (1,)), ((), ())),
+        preferred_element_type=F32,
     )
     diagonal = lane // 16 == sub
     for a in range(2):
@@ -222,18 +225,7 @@
     gram_z[z] = gram_zown[0]
 
     await_all(rec.at[pl.ds(0, nw - 1)], sem_p.at[3])
-    group = lane // 16
-    for t in range(8):
-        for c in range(2):
-            value = rec[8 * t : 8 * t + 8, c, :]
-            for bit in (1, 2, 4):
-                down = pltpu.roll(pltpu.roll(value, 8 - bit, 0), 16 * bit, 1)
-                up = pltpu.roll(pltpu.roll(value, bit, 0), 128 - 16 * bit, 1)
-                upper, right = (sub & bit) != 0, (group & bit) != 0
-                value = jnp.where(upper == right, value, jnp.where(right, down, up))
-            for e in range(2):
-                sketch_ref[8 * e + 4 * c : 8 * e + 4 * c + 4, 128 * t : 128 * t + 128] = value[4 * e : 4 * e + 4]
-
+    samples_ref[...] = rec[...]
     await_all(gram_z.at[pl.ds(0, nz - 1)], sem_g.at[1, 1])
     gram_ref[...] = jnp.sum(gram_z[...], axis=0) * gram_scale
 
@@ -248,6 +240,28 @@
     await_all(gram_z.at[pl.ds(0, nz - 1)], sem_g.at[1, 0])
 
 
+def arrange(samples_ref, total_ref, sketch_ref, gram_ref):
+    lane = lax.broadcasted_iota(jnp.int32, (8, 128), 1)
+    sub = lax.broadcasted_iota(jnp.int32, (8, 128), 0)
+    group = lane // 16
+    for t in range(8):
+        for c in range(2):
+            value = samples_ref[8 * t : 8 * t + 8, c, :]
+            for bit in (1, 2, 4):
+                down = pltpu.roll(pltpu.roll(value, 8 - bit, 0), 16 * bit, 1)
+                up = pltpu.roll(pltpu.roll(value, bit, 0), 128 - 16 * bit, 1)
+                upper, right = (sub & bit) != 0, (group & bit) != 0
+                value = jnp.where(upper == right, value, jnp.where(right, down, up))
+            for e in range(2):
+                sketch_ref[8 * e + 4 * c : 8 * e + 4 * c + 4, 128 * t : 128 * t + 128] = value[4 * e : 4 * e + 4]
+
+    for a in range(2):
+        value = jnp.broadcast_to(total_ref[a : a + 1, :], (8, 128))
+        for bit in (1, 2, 4):
+            value = jnp.where((sub & bit) != 0, pltpu.roll(value, 128 - 16 * bit, 1), value)
+        gram_ref[8 * a : 8 * a + 8, :] = value[:, :16]
+
+
 def solution(mesh):
     nw, nz = mesh.shape["wide"], mesh.shape["narrow"]
 
@@ -255,12 +269,12 @@
         cols, rows = matrix_slab.shape
         samples = sample_rows.shape[0]
         dma = pltpu.SemaphoreType.DMA
-        sketch, gram = pl.pallas_call(
+        ready, total = pl.pallas_call(
             functools.partial(
                 kernel, nw, nz, 1.0 / math.sqrt(rows * nw * nz), 1.0 / (samples * nw * nz)
             ),
             out_shape=(
-                jax.ShapeDtypeStruct((cols, samples), F32),
+                jax.ShapeDtypeStruct((nw, 2, 128), F32),
                 jax.ShapeDtypeStruct((2, 128), F32),
             ),
             in_specs=[pl.BlockSpec(memory_space=pl.ANY)] * 3,
@@ -297,7 +311,16 @@
             compiler_params=pltpu.CompilerParams(collective_id=0, has_side_effects=True),
             name="hadamard_sketch",
         )(matrix_slab, row_signs.reshape(-1, 128), sample_rows.reshape(-1, 128))
-        return sketch, gram.reshape(cols, cols)
+        return pl.pallas_call(
+            arrange,
+            out_shape=(
+                jax.ShapeDtypeStruct((cols, samples), F32),
+                jax.ShapeDtypeStruct((cols, cols), F32),
+            ),
+            in_specs=[pl.BlockSpec(memory_space=pltpu.VMEM)] * 2,
+            out_specs=[pl.BlockSpec(memory_space=pltpu.VMEM)] * 2,
+            name="arrange",
+        )(ready, total)
 
     in_specs = (P(None, ("wide", "narrow")), P(("wide", "narrow")), P(("wide", "narrow")))
     out_specs = (P(None, ("wide", "narrow")), P())

time: 54.1 us -> 52.8 us (0.976)
  local copies, waits for them, and re-layouts: 2.81 us -> 0 us
  Pallas kernels: 50.5 us -> 52 us
    unnamed x3 -> x0, local copies, waits for them, and re-layouts: 2.13 us -> none
    pallas_call x0 -> x1, Pallas kernels: none -> 1.73 us  [shards(): pl.pallas_call(arrange, out_shape=(jax.ShapeDtypeStruct((cols, samples),...]
    reshape x1 -> x0, local copies, waits for them, and re-layouts: 0.68 us -> none  [shards(): return (sketch, gram.reshape(cols, cols))]
where the time goes in v4:
time: 52.8 us; the launch traced here: 52.7 us
  Pallas kernels  52 us (98%)
  between operations  0.64 us (1%)
    pallas_call x1, Pallas kernels, shards(): pl.pallas_call(functools.partial(kernel, nw, nz, 1.0 / math.sqrt(rows * n...  50.3 us
    pallas_call x1, Pallas kernels, shards(): pl.pallas_call(arrange, out_shape=(jax.ShapeDtypeStruct((cols, samples),...  1.73 us

profile of v4, /device:TPU:1, one launch (start us, length us, event | category | flops | bytes accessed | tf_op | source)
XLA Modules:
  0.0 52.7 jit_solution(4631920598328551512)
XLA Ops:
  0.6 50.3 %hadamard_sketch.1 = (f32[64,2,128]{2,1,0:T(2,128)}, f32[2,128]{1,0:T(2,128)}) custom-call(f32[16,8192]{1,0:T(8,128)} %x_hbm.1, s32[64,128]{1,0:T(8,128)} %bitcast.2, s32[8,128]{1,0:T(8,128)} %bitcast.3), custom_call_target="tpu_custom_call" | custom-call | tf_op jit(solution)/shard_map/hadamard_sketch/pallas_call | solution.py:272
  50.9 1.7 %arrange.1 = (f32[16,1024]{1,0:T(8,128)}, f32[16,16]{1,0:T(8,128)}) custom-call(f32[64,2,128]{2,1,0:T(2,128)} %get-tuple-element.4.samples_ref, f32[2,128]{1,0:T(2,128)} %get-tuple-element.5.total_ref), custom_call_target="tpu_custom_call" | custom-call | tf_op jit(solution)/shard_map/arrange/pallas_call | solution.py:314

commit v5 on v4

--- a/solution.py
+++ b/solution.py
@@ -42,7 +42,7 @@
     x_hbm, sign_hbm, rows_hbm, samples_ref, gram_ref, x_ref, sign_ref, rows_ref,
     own, tiles, pick_own, pick_tiles, mixed, slabs, pick_z, picks,
     chosen, back, turn, ret, rec, gram_own, gram_w, gram_zown, gram_z,
-    sem_in, sem_w, sem_z, sem_p, sem_b, sem_g, sem_c,
+    late_own, late, sem_in, sem_w, sem_z, sem_p, sem_b, sem_g, sem_c,
 ):
     wide, narrow = lax.axis_index("wide"), lax.axis_index("narrow")
     w, z = lax.div(wide, 8) * 8 + narrow, lax.rem(wide, 8)
@@ -111,25 +111,36 @@
                 parts(jnp.concatenate(part, axis=0), 1), lane_table, preferred_element_type=F32
             )
             for i in range(8):
-                own[h, pl.ds(8 * (i * 8 + g), 8), :] = value[8 * i : 8 * i + 8]
-
-    def send_half(h):
+                t = i * 8 + g
+                if h == 0:
+                    own[h, pl.ds(8 * t, 8), :] = value[8 * i : 8 * i + 8]
+                    continue
+                for r in range(4):
+                    at = 8 * i + 2 * r
+                    late_own[r & 1, t, 2 * (r >> 1) : 2 * (r >> 1) + 2, :] = value[at : at + 2]
+
+    def send_half():
         mine = pl.ds(pl.multiple_of(w * 8, 8), 8)
 
         def send(p):
-            to_wide(own.at[h, pl.ds(pl.multiple_of(p * 8, 8), 8)], tiles.at[h, mine], sem_w.at[h], p)
+            to_wide(own.at[0, pl.ds(pl.multiple_of(p * 8, 8), 8)], tiles.at[mine], sem_w.at[0], p)
 
         each_wide(send)
-        tiles[h, mine, :] = own[h, mine, :]
+        tiles[mine, :] = own[0, mine, :]
+
+    def send_quarter(q):
+        each_wide(lambda p: to_wide(late_own.at[q, p], late.at[q, w], sem_w.at[1 + q], p))
+        late[q, w] = late_own[q, w]
 
     inputs[2].wait()
     inputs[0].wait()
     local(0)
     pl.semaphore_wait(barrier, nw - 1 + nz - 1)
-    send_half(0)
+    send_half()
     inputs[1].wait()
     local(1)
-    send_half(1)
+    send_quarter(0)
+    send_quarter(1)
 
     wide_table = jnp.where(lane_i // nw == row_i // nw, parity_sign(lane_i, row_i, 6), 0.0).astype(BF16)
     wide_table = jnp.concatenate([wide_table, wide_table], axis=0)
@@ -141,17 +152,26 @@
     each_wide(lambda p: to_wide(pick_own.at[lax.div(p, 8)], pick_tiles.at[w], sem_p, p))
     pick_tiles[w] = pick_own[lax.div(w, 8)]
 
-    for h in range(2):
-        await_all(tiles.at[h, pl.ds(0, 8 * (nw - 1))], sem_w.at[h, 1])
-        for p in range(4):
-            value = jnp.concatenate(
-                [tiles[h, pl.ds(4 * c + p, nw, stride=8), :] for c in range(2)], axis=0
-            )
-            value = jnp.dot(parts(value.T, 1), wide_table, preferred_element_type=F32)
-            for k in range(8):
-                mixed[h, k, 16 * p : 16 * p + 16, :] = value[16 * k : 16 * k + 16]
-        each_narrow(lambda p: to_narrow(mixed.at[h, p], slabs.at[h, z], sem_z.at[h], p))
-        slabs[h, z] = mixed[h, z]
+    def mix(h, p, halves):
+        value = jnp.concatenate(halves, axis=0)
+        value = jnp.dot(parts(value.T, 1), wide_table, preferred_element_type=F32)
+        for k in range(8):
+            mixed[h, k, 16 * p : 16 * p + 16, :] = value[16 * k : 16 * k + 16]
+
+    await_all(tiles.at[pl.ds(0, 8 * (nw - 1))], sem_w.at[0, 1])
+    for p in range(4):
+        mix(0, p, [tiles[pl.ds(4 * a + p, nw, stride=8), :] for a in range(2)])
+    each_narrow(lambda p: to_narrow(mixed.at[0, p], slabs.at[0, z], sem_z.at[0], p))
+    slabs[0, z] = mixed[0, z]
+    for q in range(2):
+        await_all(late.at[q, pl.ds(0, nw - 1)], sem_w.at[1 + q, 1])
+        for f in range(2):
+            mix(1, 2 * q + f, [late[q, :, 2 * a + f, :] for a in range(2)])
+        part = pl.ds(32 * q, 32)
+        each_narrow(
+            lambda p: to_narrow(mixed.at[1, p, part], slabs.at[1, z, part], sem_z.at[1], p)
+        )
+    slabs[1, z] = mixed[1, z]
 
     await_all(pick_tiles.at[pl.ds(0, nw - 1)], sem_p.at[1])
     gathered = pick_tiles[...].reshape(nw, 128).astype(BF16)
@@ -230,8 +250,9 @@
     gram_ref[...] = jnp.sum(gram_z[...], axis=0) * gram_scale
 
     for h in range(2):
-        await_all(tiles.at[h, pl.ds(0, 8 * (nw - 1))], sem_w.at[h, 0])
+        await_all(late.at[h, pl.ds(0, nw - 1)], sem_w.at[1 + h, 0])
         await_all(slabs.at[h, pl.ds(0, nz - 1)], sem_z.at[h, 0])
+    await_all(tiles.at[pl.ds(0, 8 * (nw - 1))], sem_w.at[0, 0])
     await_all(pick_tiles.at[pl.ds(0, nw - 1)], sem_p.at[0])
     await_all(rec.at[pl.ds(0, nw - 1)], sem_p.at[2])
     await_all(picks.at[pl.ds(0, nz - 1)], sem_c.at[0])
@@ -284,7 +305,7 @@
                 pltpu.VMEM((64, 128), jnp.int32),
                 pltpu.VMEM((8, 128), jnp.int32),
                 pltpu.VMEM((2, 8 * nw, 128), F32),
-                pltpu.VMEM((2, 8 * nw, 128), F32),
+                pltpu.VMEM((8 * nw, 128), F32),
                 pltpu.VMEM((8, 1, 128), F32),
                 pltpu.VMEM((nw, 1, 128), F32),
                 pltpu.VMEM((2, nz, 64, 128), F32),
@@ -300,8 +321,10 @@
                 pltpu.VMEM((nw, 2, 128), F32),
                 pltpu.VMEM((1, 2, 128), F32),
                 pltpu.VMEM((nz, 2, 128), F32),
+                pltpu.VMEM((2, nw, 4, 128), F32),
+                pltpu.VMEM((2, nw, 4, 128), F32),
                 dma((4,)),
-                dma((2, 2)),
+                dma((3, 2)),
                 dma((2, 2)),
                 dma((4,)),
                 dma((2,)),

time: 52.8 us -> 52.6 us (level)
  no operation moved by 1% of the time
where the time goes in v5:
time: 52.6 us; the launch traced here: 52.4 us
  Pallas kernels  51.8 us (98%)
  between operations  0.64 us (1%)
    pallas_call x1, Pallas kernels, shards(): pl.pallas_call(functools.partial(kernel, nw, nz, 1.0 / math.sqrt(rows * n...  50 us
    pallas_call x1, Pallas kernels, shards(): pl.pallas_call(arrange, out_shape=(jax.ShapeDtypeStruct((cols, samples),...  1.73 us

profile of v5, /device:TPU:1, one launch (start us, length us, event | category | flops | bytes accessed | tf_op | source)
XLA Modules:
  0.0 52.4 jit_solution(17938236310071522109)
XLA Ops:
  0.6 50.0 %hadamard_sketch.1 = (f32[64,2,128]{2,1,0:T(2,128)}, f32[2,128]{1,0:T(2,128)}) custom-call(f32[16,8192]{1,0:T(8,128)} %x_hbm.1, s32[64,128]{1,0:T(8,128)} %bitcast.2, s32[8,128]{1,0:T(8,128)} %bitcast.3), custom_call_target="tpu_custom_call" | custom-call | tf_op jit(solution)/shard_map/hadamard_sketch/pallas_call | solution.py:293
  50.7 1.7 %arrange.1 = (f32[16,1024]{1,0:T(8,128)}, f32[16,16]{1,0:T(8,128)}) custom-call(f32[64,2,128]{2,1,0:T(2,128)} %get-tuple-element.4.samples_ref, f32[2,128]{1,0:T(2,128)} %get-tuple-element.5.total_ref), custom_call_target="tpu_custom_call" | custom-call | tf_op jit(solution)/shard_map/arrange/pallas_call | solution.py:337

commit v6 on v5

--- a/solution.py
+++ b/solution.py
@@ -137,14 +137,6 @@
     local(0)
     pl.semaphore_wait(barrier, nw - 1 + nz - 1)
     send_half()
-    inputs[1].wait()
-    local(1)
-    send_quarter(0)
-    send_quarter(1)
-
-    wide_table = jnp.where(lane_i // nw == row_i // nw, parity_sign(lane_i, row_i, 6), 0.0).astype(BF16)
-    wide_table = jnp.concatenate([wide_table, wide_table], axis=0)
-
     inputs[3].wait()
     offsets = rows_ref[...].astype(F32)
     for t in range(8):
@@ -152,6 +144,14 @@
     each_wide(lambda p: to_wide(pick_own.at[lax.div(p, 8)], pick_tiles.at[w], sem_p, p))
     pick_tiles[w] = pick_own[lax.div(w, 8)]
 
+    inputs[1].wait()
+    local(1)
+    send_quarter(0)
+    send_quarter(1)
+
+    wide_table = jnp.where(lane_i // nw == row_i // nw, parity_sign(lane_i, row_i, 6), 0.0).astype(BF16)
+    wide_table = jnp.concatenate([wide_table, wide_table], axis=0)
+
     def mix(h, p, halves):
         value = jnp.concatenate(halves, axis=0)
         value = jnp.dot(parts(value.T, 1), wide_table, preferred_element_type=F32)
@@ -163,16 +163,6 @@
         mix(0, p, [tiles[pl.ds(4 * a + p, nw, stride=8), :] for a in range(2)])
     each_narrow(lambda p: to_narrow(mixed.at[0, p], slabs.at[0, z], sem_z.at[0], p))
     slabs[0, z] = mixed[0, z]
-    for q in range(2):
-        await_all(late.at[q, pl.ds(0, nw - 1)], sem_w.at[1 + q, 1])
-        for f in range(2):
-            mix(1, 2 * q + f, [late[q, :, 2 * a + f, :] for a in range(2)])
-        part = pl.ds(32 * q, 32)
-        each_narrow(
-            lambda p: to_narrow(mixed.at[1, p, part], slabs.at[1, z, part], sem_z.at[1], p)
-        )
-    slabs[1, z] = mixed[1, z]
-
     await_all(pick_tiles.at[pl.ds(0, nw - 1)], sem_p.at[1])
     gathered = pick_tiles[...].reshape(nw, 128).astype(BF16)
     gathered = jnp.concatenate([gathered, gathered], axis=0)
@@ -185,6 +175,16 @@
         pick_z[k] = by_run[2 * k : 2 * k + 2]
     each_narrow(lambda p: to_narrow(pick_z.at[p], picks.at[z], sem_c, p))
     picks[z] = pick_z[z]
+
+    for q in range(2):
+        await_all(late.at[q, pl.ds(0, nw - 1)], sem_w.at[1 + q, 1])
+        for f in range(2):
+            mix(1, 2 * q + f, [late[q, :, 2 * a + f, :] for a in range(2)])
+        part = pl.ds(32 * q, 32)
+        each_narrow(
+            lambda p: to_narrow(mixed.at[1, p, part], slabs.at[1, z, part], sem_z.at[1], p)
+        )
+    slabs[1, z] = mixed[1, z]
 
     await_all(picks.at[pl.ds(0, nz - 1)], sem_c.at[1])
     place = lax.broadcasted_iota(jnp.int32, (8, 128), 0).astype(F32)

time: 52.6 us -> 52.5 us (level)
  no operation moved by 1% of the time
where the time goes in v6:
time: 52.5 us; the launch traced here: 52.3 us
  Pallas kernels  51.7 us (98%)
  between operations  0.64 us (1%)
    pallas_call x1, Pallas kernels, shards(): pl.pallas_call(functools.partial(kernel, nw, nz, 1.0 / math.sqrt(rows * n...  50 us
    pallas_call x1, Pallas kernels, shards(): pl.pallas_call(arrange, out_shape=(jax.ShapeDtypeStruct((cols, samples),...  1.73 us

profile of v6, /device:TPU:1, one launch (start us, length us, event | category | flops | bytes accessed | tf_op | source)
XLA Modules:
  0.0 52.3 jit_solution(7529231019991065753)
XLA Ops:
  0.6 50.0 %hadamard_sketch.1 = (f32[64,2,128]{2,1,0:T(2,128)}, f32[2,128]{1,0:T(2,128)}) custom-call(f32[16,8192]{1,0:T(8,128)} %x_hbm.1, s32[64,128]{1,0:T(8,128)} %bitcast.2, s32[8,128]{1,0:T(8,128)} %bitcast.3), custom_call_target="tpu_custom_call" | custom-call | tf_op jit(solution)/shard_map/hadamard_sketch/pallas_call | solution.py:293
  50.6 1.7 %arrange.1 = (f32[16,1024]{1,0:T(8,128)}, f32[16,16]{1,0:T(8,128)}) custom-call(f32[64,2,128]{2,1,0:T(2,128)} %get-tuple-element.4.samples_ref, f32[2,128]{1,0:T(2,128)} %get-tuple-element.5.total_ref), custom_call_target="tpu_custom_call" | custom-call | tf_op jit(solution)/shard_map/arrange/pallas_call | solution.py:337
